TPU v7x, 256 devices: a whole 4x4x8 slice. The times are simulated.
256 devices in a mesh: seq: 32 (over x, y, core), head: 8 (over z).
Axes of the slice: x: 4, y: 4, z: 8, core: 2. Of those that a mesh axis runs over, the one named last changes fastest.
Arguments:
- new_states: bfloat16 [96, 1024], replicated, may hold values from -6 to 6
- lengths: int32 [24], replicated, may hold values from 1 to 16380, as said below
- cache_keys: bfloat16 [24, 16384, 1024], P(None, 'seq', 'head'), may hold values from -3000 to 3000
- cache_values: bfloat16 [24, 16384, 1024], P(None, 'seq', 'head'), may hold values from -6 to 6
- buckets: int32 [24, 4, 16384], P(None, None, 'seq'), may hold values from 0 to 31, as said below
- attn_gain: float32 [1024], replicated, may hold values from 0.25 to 1.75
- w_query: bfloat16 [1024, 1024], P(None, 'head'), may hold values from -0.0234375 to 0.0234375
- w_key: bfloat16 [1024, 1024], P(None, 'head'), may hold values from -0.1875 to 0.1875
- w_value: bfloat16 [1024, 1024], P(None, 'head'), may hold values from -0.1875 to 0.1875
- rel_bias: float32 [32, 16], P(None, 'head'), may hold values from -27 to 2
- w_out: bfloat16 [1024, 1024], P('head'), may hold values from -0.1875 to 0.1875
- ffn_gain: float32 [1024], replicated, may hold values from 0.25 to 1.75
- w_router: float32 [1024, 16], replicated, may hold values from -0.1875 to 0.1875
- w_gate: bfloat16 [16, 1024, 2816], P('head', None, 'seq'), may hold values from -0.1875 to 0.1875
- w_up: bfloat16 [16, 1024, 2816], P('head', None, 'seq'), may hold values from -0.1875 to 0.1875
- w_down: bfloat16 [16, 2816, 1024], P('head', 'seq'), may hold values from -0.109375 to 0.109375
- expert_picks: int32 [4, 24, 2], replicated, may hold values from 0 to 15, all different within a row; in each aligned block of 24 rows (0 to 23, 24 to 47, ..., all dimensions but the last counted through in order) at most 4 rows name the same one
- final_gain: float32 [1024], replicated, may hold values from 0.25 to 1.75
- w_vocab: bfloat16 [1024, 32128], P(None, 'seq'), may hold values from -0.5 to 0.5
Outputs:
- final_hidden: bfloat16 [96, 1024], P('head')
- hidden_norm: float32 [96], P('head')
- logit_max: float32 [96], P('head')
Inputs may be any that keep to these rules, and one draw needn't show every extreme that they name: `lengths`: some request has exactly 16380 cached positions. buckets[r, t, p] is the T5 relative position bucket (16 exact buckets, then logarithmic up to a distance of 128) of the distance lengths[r] + t - p where that is not negative, else 0. `expert_picks`: A request's two picks at a step differ; at each step no expert is picked by more than 4 requests, a bound that some block reaches.
All inputs are finite; a program needn't handle non-finite values.
Results may differ from a plain program's by a relative error of at most 0.0096.
Values may be sent and summed in bfloat16 or wider, within the bound.
A program may use at most 64 MiB of HBM per device.

v0:
```python
import jax
import jax.numpy as jnp
from jax import lax
from jax.sharding import PartitionSpec as P

CAP = 4


def joined(part, axis, combine):
    gathered = jax.tree.map(lambda a: lax.all_gather(a, axis), part)

    def take(source):
        return jax.tree.map(lambda a: lax.dynamic_index_in_dim(a, source, 0, False), gathered)

    return lax.fori_loop(
        1, lax.axis_size(axis), lambda source, state: combine(state, take(source)), take(0)
    )


def norm_parts(values, gain_row):
    norm_root = jnp.sqrt(jnp.mean(values * values, axis=-1, keepdims=True) + 1e-06)
    return (values / norm_root * gain_row, norm_root[..., 0])


def join_three(earlier_part, later_part):
    joint_top = jnp.maximum(earlier_part[0], later_part[0])
    lead_scale = jnp.exp(earlier_part[0] - joint_top)
    trail_scale = jnp.exp(later_part[0] - joint_top)
    mass = earlier_part[1] * lead_scale + later_part[1] * trail_scale
    weighted = earlier_part[2] * lead_scale[..., None] + later_part[2] * trail_scale[..., None]
    return (joint_top, mass, weighted)


def shards(
    new_states,
    lengths,
    cache_keys,
    cache_values,
    buckets,
    attn_gain,
    w_query,
    w_key,
    w_value,
    rel_bias,
    w_out,
    ffn_gain,
    w_router,
    w_gate,
    w_up,
    w_down,
    expert_picks,
    final_gain,
    w_vocab,
):
    seq_count = lax.axis_size("seq")
    head_count = lax.axis_size("head")
    seq_index = lax.axis_index("seq")
    head_index = lax.axis_index("head")
    requests, span_local, inner_local = cache_keys.shape
    tokens = new_states.shape[0]
    step_count = tokens // requests
    bucket_count, heads_local = rel_bias.shape
    head_dim = inner_local // heads_local
    states = new_states.astype(jnp.float32)
    scaled, _ = norm_parts(states, attn_gain)
    scaled = scaled.astype(jnp.bfloat16)
    queries = (
        jnp.dot(scaled, w_query, preferred_element_type=jnp.float32)
        .astype(jnp.bfloat16)
        .reshape(requests, step_count, heads_local, head_dim)
    )
    key_new = (
        jnp.dot(scaled, w_key, preferred_element_type=jnp.float32)
        .astype(jnp.bfloat16)
        .reshape(requests, step_count, inner_local)
    )
    value_new = (
        jnp.dot(scaled, w_value, preferred_element_type=jnp.float32)
        .astype(jnp.bfloat16)
        .reshape(requests, step_count, inner_local)
    )
    position = seq_index * span_local + jnp.arange(span_local, dtype=jnp.int32)
    target = lengths[:, None] + jnp.arange(step_count, dtype=jnp.int32)[None, :]
    landing = position[None, None, :] == target[:, :, None]
    landed = jnp.any(landing, axis=1)[:, :, None]
    landing_low = landing.astype(jnp.bfloat16)
    placed_keys = jnp.einsum(
        "rtp,rtc->rpc", landing_low, key_new, preferred_element_type=jnp.float32
    ).astype(jnp.bfloat16)
    placed_values = jnp.einsum(
        "rtp,rtc->rpc", landing_low, value_new, preferred_element_type=jnp.float32
    ).astype(jnp.bfloat16)
    key_rows = jnp.where(landed, placed_keys, cache_keys).reshape(
        requests, span_local, heads_local, head_dim
    )
    value_rows = jnp.where(landed, placed_values, cache_values).reshape(
        requests, span_local, heads_local, head_dim
    )
    scores = jnp.einsum("rthd,rphd->rthp", queries, key_rows, preferred_element_type=jnp.float32)
    bucket_hot = (buckets[..., None] == jnp.arange(bucket_count, dtype=jnp.int32)).astype(
        jnp.float32
    )
    scores = scores + jnp.einsum(
        "rtpb,bh->rthp", bucket_hot, rel_bias, precision=lax.Precision.HIGHEST
    )
    allowed = (position[None, None, :] <= target[:, :, None])[:, :, None, :]
    scores = jnp.where(allowed, scores, -1e30)
    local_top = jnp.max(scores, axis=-1)
    weights = jnp.where(allowed, jnp.exp(scores - local_top[..., None]), 0.0)
    local_mass = jnp.sum(weights, axis=-1)
    partial_value = jnp.einsum(
        "rthp,rphd->rthd", weights, value_rows.astype(jnp.float32), precision=lax.Precision.HIGHEST
    )
    out_rows = w_out.astype(jnp.float32)
    global_top, global_mass, summed = joined(
        (local_top, local_mass, partial_value), "seq", join_three
    )
    heads_out = (summed / global_mass[..., None]).reshape(tokens, inner_local)
    projected = jnp.dot(heads_out, out_rows, precision=lax.Precision.HIGHEST)
    mixed_rows = lax.psum(projected, "head")
    hidden_one = states + mixed_rows
    normed, _ = norm_parts(hidden_one, ffn_gain)
    router_logits = jnp.dot(normed, w_router, precision=lax.Precision.HIGHEST)
    normed_low = normed.astype(jnp.bfloat16)
    expert_total = w_router.shape[1]
    local_experts, model_width, units_local = w_gate.shape
    expert_ids = jnp.arange(expert_total, dtype=jnp.int32)
    pick_marks = (expert_picks[..., None] == expert_ids).astype(jnp.int32)
    per_step = jnp.sum(pick_marks, axis=2)
    earlier = jnp.cumsum(per_step, axis=1) - per_step
    slot_index = jnp.sum(pick_marks * earlier[:, :, None, :], axis=-1)
    pick_total = expert_picks.shape[2]
    token_picks = jnp.transpose(expert_picks, (1, 0, 2)).reshape(tokens, pick_total)
    token_slots = jnp.transpose(slot_index, (1, 0, 2)).reshape(tokens, pick_total)
    token_steps = jnp.arange(tokens, dtype=jnp.int32) % step_count
    picked = jnp.sum(
        jnp.where(token_picks[..., None] == expert_ids, router_logits[:, None, :], 0.0), axis=-1
    )
    gate_first = jax.nn.sigmoid(picked[:, 0] - picked[:, 1])
    gate_second = jax.nn.sigmoid(picked[:, 1] - picked[:, 0])
    slot_rows = step_count * CAP
    row_ids = jnp.arange(local_experts * slot_rows, dtype=jnp.int32)
    row_expert = head_index * local_experts + row_ids // slot_rows
    row_step = row_ids // CAP % step_count
    row_slot = row_ids % CAP
    chooser = jnp.zeros((row_ids.shape[0], tokens), jnp.float32)
    for pick_rank in range(pick_total):
        matched = (
            (row_expert[:, None] == token_picks[None, :, pick_rank])
            & (row_step[:, None] == token_steps[None, :])
            & (row_slot[:, None] == token_slots[None, :, pick_rank])
        )
        chooser = chooser + matched.astype(jnp.float32)
    routed = jnp.dot(
        chooser.astype(jnp.bfloat16), normed_low, preferred_element_type=jnp.float32
    ).astype(jnp.bfloat16)
    routed = routed.reshape(local_experts, slot_rows, model_width)
    gate_part = jnp.einsum("esd,edf->esf", routed, w_gate, preferred_element_type=jnp.float32)
    up_part = jnp.einsum("esd,edf->esf", routed, w_up, preferred_element_type=jnp.float32)
    hidden_units = (jax.nn.gelu(gate_part, approximate=True) * up_part).astype(jnp.bfloat16)
    down_part = jnp.einsum("esf,efd->esd", hidden_units, w_down, preferred_element_type=jnp.float32)
    expert_share = lax.psum_scatter(down_part, "seq", scatter_dimension=2, tiled=True).astype(
        jnp.bfloat16
    )
    share_width = expert_share.shape[2]
    collected = lax.all_gather(expert_share[None], ("seq", "head"), axis=0, tiled=True)
    arranged = collected.reshape(seq_count, head_count, local_experts, slot_rows, share_width)
    arranged = jnp.transpose(arranged, (1, 2, 3, 0, 4)).reshape(
        expert_total * slot_rows, seq_count * share_width
    )
    group_size = tokens // head_count
    first_row = head_index * group_size
    own_picks = lax.dynamic_slice_in_dim(token_picks, first_row, group_size, 0)
    own_slots = lax.dynamic_slice_in_dim(token_slots, first_row, group_size, 0)
    own_steps = lax.dynamic_slice_in_dim(token_steps, first_row, group_size, 0)
    own_first = lax.dynamic_slice_in_dim(gate_first, first_row, group_size, 0)
    own_second = lax.dynamic_slice_in_dim(gate_second, first_row, group_size, 0)
    own_hidden = lax.dynamic_slice_in_dim(hidden_one, first_row, group_size, 0)
    flat_rows = own_picks * slot_rows + own_steps[:, None] * CAP + own_slots
    every_row = jnp.arange(expert_total * slot_rows, dtype=jnp.int32)
    select_first = (flat_rows[:, 0:1] == every_row[None, :]).astype(jnp.bfloat16)
    select_second = (flat_rows[:, 1:2] == every_row[None, :]).astype(jnp.bfloat16)
    expert_mix = own_first[:, None] * jnp.dot(
        select_first, arranged, preferred_element_type=jnp.float32
    )
    expert_mix = expert_mix + own_second[:, None] * jnp.dot(
        select_second, arranged, preferred_element_type=jnp.float32
    )
    final_rows = (own_hidden + expert_mix).astype(jnp.bfloat16)
    scaled_out, norm_root = norm_parts(final_rows.astype(jnp.float32), final_gain)
    logits = jnp.dot(scaled_out.astype(jnp.bfloat16), w_vocab, preferred_element_type=jnp.float32)
    top_logit = lax.pmax(jnp.max(logits, axis=-1), "seq")
    return (final_rows, norm_root, top_logit)


def solution(mesh):
    placed = (
        P(),
        P(),
        P(None, "seq", "head"),
        P(None, "seq", "head"),
        P(None, None, "seq"),
        P(),
        P(None, "head"),
        P(None, "head"),
        P(None, "head"),
        P(None, "head"),
        P("head", None),
        P(),
        P(),
        P("head", None, "seq"),
        P("head", None, "seq"),
        P("head", "seq", None),
        P(),
        P(),
        P(None, "seq"),
    )
    return jax.shard_map(
        shards,
        mesh=mesh,
        in_specs=placed,
        out_specs=(P("head", None), P("head"), P("head")),
        check_vma=False,
    )
```

profile of v0, /device:TPU:32, one launch (start us, length us, event | category | flops | bytes accessed | tf_op | source)
XLA Modules:
  0.0 482.6 jit_solution(6117893066806250847)
XLA Ops:
  7.3 1.2 fusion.13
  8.5 0.7 iota_add_fusion
  9.2 1.3 convolution_convert_fusion.2
  10.7 1.3 convolution_convert_fusion.1
  12.3 4.6 copy.74
  17.0 4.7 copy.77
  22.0 2.0 fusion.4
  24.0 3.1 convert_select_fusion.1
  27.1 1.0 convert_select_fusion
  28.8 3.3 convolution_bitcast_fusion.1
  33.2 25.3 %all-gather.1 = f32[768,4,2]{1,2,0:T(2,128)S(1)} all-gather(f32[24,4,2]{1,2,0:T(2,128)S(1)} %fusion.16), channel_id=3, replica_groups=mesh['seq'=32,'head'=8] {'seq'}, dimensions={0}, use_global_device_ids=true | all-gather | bytes 25344 | tf_op jit(solution)/shard_map/all_gather | solution.py:10
  59.2 25.2 %all-gather = f32[768,4,2]{1,2,0:T(2,128)S(1)} all-gather(f32[24,4,2]{1,2,0:T(2,128)S(1)} %get-tuple-element.240), channel_id=2, replica_groups=mesh['seq'=32,'head'=8] {'seq'}, dimensions={0}, use_global_device_ids=true | all-gather | bytes 25344 | tf_op jit(solution)/shard_map/all_gather | solution.py:10
  84.4 1.2 copy.83
  86.0 0.9 slice.42
  87.0 76.0 %while.19 = (s32[]{:T(128)}, f32[24,4,2]{0,2,1:T(2,128)S(1)}, f32[24,4,2]{0,2,1:T(2,128)S(1)}, f32[24,4,2,64]{3,2,1,0:T(2,128)S(1)}, f32[32,24,4,2]{1,3,2,0:T(2,...) while((s32[]{:T(128)}, f32[24,4,2]{0,2,1:T(2,128)S(1)}, ...), condition=%wide.region_5.6_spmd, body=%wide.region_4.5_spmd.sunk | while | flops 38021 | bytes 256655 | solution.py:15
  87.9 0.9 constant_dynamic-slice_fusion.6
  90.4 0.9 constant_dynamic-slice_fusion.6
  92.8 0.9 constant_dynamic-slice_fusion.6
  95.3 0.9 constant_dynamic-slice_fusion.6
  97.7 0.9 constant_dynamic-slice_fusion.6
  100.2 0.9 constant_dynamic-slice_fusion.6
  101.7 0.7 fusion.99
  102.6 0.9 constant_dynamic-slice_fusion.6
  105.1 0.9 constant_dynamic-slice_fusion.6
  107.6 0.9 constant_dynamic-slice_fusion.6
  110.0 0.9 constant_dynamic-slice_fusion.6
  112.5 0.9 constant_dynamic-slice_fusion.6
  114.9 0.9 constant_dynamic-slice_fusion.6
  117.4 0.9 constant_dynamic-slice_fusion.6
  119.8 0.9 constant_dynamic-slice_fusion.6
  121.4 0.7 fusion.99
  122.3 0.9 constant_dynamic-slice_fusion.6
  124.7 0.9 constant_dynamic-slice_fusion.6
  127.2 0.9 constant_dynamic-slice_fusion.6
  129.6 0.9 constant_dynamic-slice_fusion.6
  132.1 0.9 constant_dynamic-slice_fusion.6
  134.5 0.9 constant_dynamic-slice_fusion.6
  137.0 0.9 constant_dynamic-slice_fusion.6
  138.5 0.7 fusion.99
  139.4 0.9 constant_dynamic-slice_fusion.6
  141.9 0.9 constant_dynamic-slice_fusion.6
  144.3 0.9 constant_dynamic-slice_fusion.6
  146.8 0.9 constant_dynamic-slice_fusion.6
  149.2 0.9 constant_dynamic-slice_fusion.6
  151.7 0.9 constant_dynamic-slice_fusion.6
  154.1 0.9 constant_dynamic-slice_fusion.6
  156.6 0.9 constant_dynamic-slice_fusion.6
  158.1 0.7 fusion.99
  159.0 0.9 constant_dynamic-slice_fusion.6
  161.5 0.9 constant_dynamic-slice_fusion.6
  163.4 1.1 fusion.77
  164.6 72.5 %all-reduce.2.cloned.1.call-done = f32[96,1024]{1,0:T(8,128)} async-done(((f32[96,1024]{1,0:T(8,128)}), f32[96,1024]{1,0:T(8,128)}) %all-reduce.2.cloned.1.call-update) | async-done | bytes 393232 | tf_op jit(solution)/shard_map/psum | solution.py:120
  237.1 1.1 multiply_reduce_fusion
  239.1 1.2 fusion.78
  240.3 2.0 fusion.12
  242.3 1.3 copy.98
  243.6 1.4 reshape.208
  245.2 83.7 %reduce-scatter.4.cloned.1.call-done = f32[32,32]{1,0:T(8,128)} async-done(((f32[1024,32]{1,0:T(8,128)}), f32[32,32]{1,0:T(8,128)}) %reduce-scatter.4.cloned.1.call-update) | async-done | bytes 4112
  328.9 0.8 reshape.209
  329.8 73.4 %all-gather.3 = bf16[512,16,32]{2,1,0:T(8,128)(2,1)S(1)} all-gather(bf16[2,16,32]{2,1,0:T(8,128)(2,1)S(1)} %copy.99), channel_id=5, replica_groups=mesh['seq'=32,'head'=8] {'seq','head'}, dimensions={0}, use_global_device_ids=true | all-gather | bytes 526336 | tf_op jit(solution)/shard_map/all_gather | solution.py:166
  403.2 2.7 copy.112
  405.9 3.5 reshape.189
  410.0 0.8 convolution_reduce_fusion
  410.8 65.3 %pmax.7 = f32[12]{0:T(128)} all-reduce(f32[12]{0:T(128)S(1)} %convolution_reduce_fusion), channel_id=1, replica_groups=mesh['seq'=32,'head'=8] {'seq'}, use_global_device_ids=true, to_apply=%region_15.16 | all-reduce | flops 12 | bytes 96 | tf_op jit(solution)/shard_map/pmax | solution.py:192
  (201 shorter events, 50.4 us)
Async XLA Ops:
  7.2 402.9 %copy-start = (bf16[1024,1004]{0,1:T(8,128)(2,1)S(1)}, bf16[1024,1004]{0,1:T(8,128)(2,1)}, u32[]{:S(2)}) copy-start(bf16[1024,1004]{0,1:T(8,128)(2,1)} %param.39) | copy-start | bytes 6168580
  7.2 4.8 copy-start.2
  7.2 4.8 copy-start.12
  7.2 4.8 copy-start.9
  7.2 78.8 %all-gather.6.cloned.1.call-start = ((), (), s32[]{:S(2)}) async-start(), calls=%async_computation.2 | async-start | bytes 3244032 | tf_op jit(solution)/shard_map/all_gather | solution.py:10
  16.9 5.0 %copy-start.10 = (s32[24,4,512]{2,1,0:T(4,128)S(1)}, s32[24,4,512]{2,1,0:T(4,128)}, u32[]{:S(2)}) copy-start(s32[24,4,512]{2,1,0:T(4,128)} %param.25) | copy-start | bytes 589828
  17.0 5.0 %copy-start.14 = (f32[32,2]{0,1:T(2,128)S(1)}, f32[32,2]{0,1:T(2,128)}, u32[]{:S(2)}) copy-start(f32[32,2]{0,1:T(2,128)} %param.30) | copy-start | bytes 772
  24.0 3.1 copy-start.1
  28.8 3.3 copy-start.6
  32.1 205.0 %all-reduce.2.cloned.1.call-start = ((), (), s32[]{:S(2)}) async-start(), calls=%async_computation.1 | async-start | bytes 786432 | tf_op jit(solution)/shard_map/psum | solution.py:120
  59.1 104.3 %copy-start.4 = (bf16[128,1024]{1,0:T(8,128)(2,1)S(1)}, bf16[128,1024]{1,0:T(8,128)(2,1)}, u32[]{:S(2)}) copy-start(bf16[128,1024]{1,0:T(8,128)(2,1)} %param.31) | copy-start | bytes 786436
  86.9 151.3 %copy-start.11 = (f32[1024,16]{0,1:T(8,128)S(1)}, f32[1024,16]{0,1:T(8,128)}, u32[]{:S(2)}) copy-start(f32[1024,16]{0,1:T(8,128)} %param.33) | copy-start | bytes 196612
  87.0 151.3 %copy-start.13 = (f32[1024]{0:T(1024)S(1)}, f32[1024]{0:T(1024)}, u32[]{:S(2)}) copy-start(f32[1024]{0:T(1024)} %param.32) | copy-start | bytes 12292
  163.0 77.3 %copy-start.3 = (bf16[2,88,1024]{2,1,0:T(8,128)(2,1)S(1)}, bf16[2,88,1024]{2,1,0:T(8,128)(2,1)}, u32[]{:S(2)}) copy-start(bf16[2,88,1024]{2,1,0:T(8,128)(2,1)} %param.36) | copy-start | bytes 1081348
  164.5 164.3 %reduce-scatter.4.cloned.1.call-start = ((), (), s32[]{:S(2)}) async-start(), calls=%async_computation.3 | async-start | bytes 540672
  403.2 6.8 %copy-start.7 = (f32[1024]{0:T(1024)S(1)}, f32[1024]{0:T(1024)}, u32[]{:S(2)}) copy-start(f32[1024]{0:T(1024)} %param.38) | copy-start | bytes 12292
  410.0 66.1 %copy-start.5 = (bf16[12,1024]{1,0:T(8,128)(2,1)}, bf16[12,1024]{1,0:T(8,128)(2,1)S(1)}, u32[]{:S(2)}) copy-start(bf16[12,1024]{1,0:T(8,128)(2,1)S(1)} %get-tuple-element.243) | copy-start | bytes 73732
  410.0 66.1 %copy-start.8 = (f32[12]{0:T(128)}, f32[12]{0:T(128)S(1)}, u32[]{:S(2)}) copy-start(f32[12]{0:T(128)S(1)} %add_sqrt_fusion) | copy-start | bytes 148
Sparse Core Ops, SparseCore 0:
  32.2 53.7 all-gather.5
  164.6 72.4 all-reduce.1
  245.2 83.6 reduce-scatter.3
where the time goes:
time: 485 us; the launch traced here: 483 us
  blocking collectives  189 us (39%)
  waiting for transfers between devices  156 us (32%)
  local copies, waits for them, and re-layouts  58.1 us (12%)
  other arithmetic  44.9 us (9%)
  matrix products  19.3 us (4%)
  between operations  14.1 us (3%)
    unnamed x4, waiting for transfers between devices  83.7 us
    all_gather x1, blocking collectives, shards(): lax.all_gather(expert_share[None], ('seq', 'head'), axis=0, tiled=True)  73.4 us
    psum x1, waiting for transfers between devices, shards(): mixed_rows = lax.psum(projected, 'head')  72.5 us
    pmax x1, blocking collectives, shards(): top_logit = lax.pmax(jnp.max(logits, axis=-1), 'seq')  65.3 us
    all_gather x2, blocking collectives, joined(): gathered = jax.tree.map(lambda a: lax.all_gather(a, axis), part)  50.5 us
    dynamic_slice x34, local copies, waits for them, and re-layouts, take(): lax.dynamic_index_in_dim(a, source, 0, False)  28.9 us
    add x31, other arithmetic, join_three(): mass = earlier_part[1] * lead_scale + later_part[1] * trail_scale  21.9 us
    add x31, other arithmetic, join_three(): earlier_part[2] * lead_scale[..., None]  18.8 us
  transfers between devices with their start and end apart: 3, of which 3 were waited for; matrix products, arithmetic and copies ran while one was open for 1% of the time, Pallas kernels for 0%

commit v1 on v0

--- a/solution.py
+++ b/solution.py
@@ -163,7 +163,13 @@
         jnp.bfloat16
     )
     share_width = expert_share.shape[2]
-    collected = lax.all_gather(expert_share[None], ("seq", "head"), axis=0, tiled=True)
+    body = expert_share[None]
+    collected = jnp.concatenate(
+        lax.all_to_all(
+            jnp.stack([body] * lax.psum(1, ("seq", "head")), axis=0), ("seq", "head"), 0, 0
+        ),
+        axis=0,
+    )
     arranged = collected.reshape(seq_count, head_count, local_experts, slot_rows, share_width)
     arranged = jnp.transpose(arranged, (1, 2, 3, 0, 4)).reshape(
         expert_total * slot_rows, seq_count * share_width

time: 485 us -> 453 us (0.934)
  blocking collectives: 189 us -> 114 us
  waiting for transfers between devices: 156 us -> 177 us
  starting transfers between devices: 0.12 us -> 11.3 us
  local copies, waits for them, and re-layouts: 58.1 us -> 67.5 us
    all_gather x1 -> x0, blocking collectives: 73.4 us -> none  [shards(): lax.all_gather(expert_share[None], ('seq', 'head'), axis=0, tiled=True)]
    all_to_all x0 -> x1, waiting for transfers between devices: none -> 20 us  [shards(): lax.all_to_all(jnp.stack([body] * lax.psum(1, ('seq', 'head')), axis=0),...]
    all_to_all x0 -> x1, starting transfers between devices: none -> 11.2 us  [shards(): lax.all_to_all(jnp.stack([body] * lax.psum(1, ('seq', 'head')), axis=0),...]
    unnamed x36 -> x38, local copies, waits for them, and re-layouts: 13.1 us -> 19.4 us
  transfers between devices with their start and end apart: 3 -> 4, of which waited for: 3 -> 4; matrix products, arithmetic and copies ran while one was open for 1% -> 1% of each run, Pallas kernels for 0% -> 0%
where the time goes in v1:
time: 453 us; the launch traced here: 449 us
  waiting for transfers between devices  177 us (39%)
  blocking collectives  114 us (25%)
  local copies, waits for them, and re-layouts  67.5 us (15%)
  other arithmetic  44.9 us (10%)
  matrix products  19.3 us (4%)
  between operations  14.1 us (3%)
  starting transfers between devices  11.3 us (2%)
    unnamed x4, waiting for transfers between devices  83.8 us
    psum x1, waiting for transfers between devices, shards(): mixed_rows = lax.psum(projected, 'head')  72.9 us
    pmax x1, blocking collectives, shards(): top_logit = lax.pmax(jnp.max(logits, axis=-1), 'seq')  63.6 us
    all_gather x2, blocking collectives, joined(): gathered = jax.tree.map(lambda a: lax.all_gather(a, axis), part)  50.5 us
    dynamic_slice x34, local copies, waits for them, and re-layouts, take(): lax.dynamic_index_in_dim(a, source, 0, False)  28.9 us
    add x31, other arithmetic, join_three(): mass = earlier_part[1] * lead_scale + later_part[1] * trail_scale  21.9 us
    all_to_all x1, waiting for transfers between devices, shards(): lax.all_to_all(jnp.stack([body] * lax.psum(1, ('seq', 'head')), axis=0),...  20 us
    unnamed x38, local copies, waits for them, and re-layouts  19.4 us
  transfers between devices with their start and end apart: 4, of which 4 were waited for; matrix products, arithmetic and copies ran while one was open for 1% of the time, Pallas kernels for 0%

profile of v1, /device:TPU:32, one launch (start us, length us, event | category | flops | bytes accessed | tf_op | source)
XLA Modules:
  0.0 448.8 jit_solution(6325501579947893515)
XLA Ops:
  7.3 1.2 fusion.13
  8.5 0.7 iota_add_fusion
  9.2 1.3 convolution_convert_fusion.2
  10.7 1.3 convolution_convert_fusion.1
  12.3 4.6 %copy.90 = bf16[24,512,128]{1,2,0:T(8,128)(2,1)} copy(bf16[24,512,128]{2,1,0:T(8,128)(2,1)} %param.23) | data formatting | bytes 6291456 | tf_op args[2]
  17.0 4.7 %copy.93 = bf16[24,512,128]{1,2,0:T(8,128)(2,1)} copy(bf16[24,512,128]{2,1,0:T(8,128)(2,1)} %param.24) | data formatting | bytes 6291456 | tf_op args[3]
  22.0 2.0 fusion.4
  24.0 3.1 convert_select_fusion.1
  27.1 1.0 convert_select_fusion
  28.8 3.3 convolution_bitcast_fusion.1
  33.2 25.3 %all-gather.1 = f32[768,4,2]{1,2,0:T(2,128)S(1)} all-gather(f32[24,4,2]{1,2,0:T(2,128)S(1)} %fusion.16), channel_id=3, replica_groups=mesh['seq'=32,'head'=8] {'seq'}, dimensions={0}, use_global_device_ids=true | all-gather | bytes 25344 | tf_op jit(solution)/shard_map/all_gather | solution.py:10
  59.1 25.2 %all-gather = f32[768,4,2]{1,2,0:T(2,128)S(1)} all-gather(f32[24,4,2]{1,2,0:T(2,128)S(1)} %get-tuple-element.247), channel_id=2, replica_groups=mesh['seq'=32,'head'=8] {'seq'}, dimensions={0}, use_global_device_ids=true | all-gather | bytes 25344 | tf_op jit(solution)/shard_map/all_gather | solution.py:10
  84.4 1.2 copy.99
  86.0 0.9 slice.42
  87.0 76.0 %while.19 = (s32[]{:T(128)}, f32[24,4,2]{0,2,1:T(2,128)S(1)}, f32[24,4,2]{0,2,1:T(2,128)S(1)}, f32[24,4,2,64]{3,2,1,0:T(2,128)S(1)}, f32[32,24,4,2]{1,3,2,0:T(2,...) while((s32[]{:T(128)}, f32[24,4,2]{0,2,1:T(2,128)S(1)}, ...), condition=%wide.region_5.6_spmd, body=%wide.region_4.5_spmd.sunk | while | flops 38021 | bytes 256655 | solution.py:15
  87.9 0.9 constant_dynamic-slice_fusion.6
  90.4 0.9 constant_dynamic-slice_fusion.6
  92.8 0.9 constant_dynamic-slice_fusion.6
  95.3 0.9 constant_dynamic-slice_fusion.6
  97.7 0.9 constant_dynamic-slice_fusion.6
  100.2 0.9 constant_dynamic-slice_fusion.6
  102.6 0.9 constant_dynamic-slice_fusion.6
  105.1 0.9 constant_dynamic-slice_fusion.6
  107.5 0.9 constant_dynamic-slice_fusion.6
  110.0 0.9 constant_dynamic-slice_fusion.6
  112.4 0.9 constant_dynamic-slice_fusion.6
  114.9 0.9 constant_dynamic-slice_fusion.6
  117.4 0.9 constant_dynamic-slice_fusion.6
  119.8 0.9 constant_dynamic-slice_fusion.6
  122.3 0.9 constant_dynamic-slice_fusion.6
  124.7 0.9 constant_dynamic-slice_fusion.6
  127.2 0.9 constant_dynamic-slice_fusion.6
  129.6 0.9 constant_dynamic-slice_fusion.6
  132.1 0.9 constant_dynamic-slice_fusion.6
  134.5 0.9 constant_dynamic-slice_fusion.6
  136.9 0.9 constant_dynamic-slice_fusion.6
  139.4 0.9 constant_dynamic-slice_fusion.6
  141.9 0.9 constant_dynamic-slice_fusion.6
  144.3 0.9 constant_dynamic-slice_fusion.6
  146.8 0.9 constant_dynamic-slice_fusion.6
  149.2 0.9 constant_dynamic-slice_fusion.6
  151.7 0.9 constant_dynamic-slice_fusion.6
  154.1 0.9 constant_dynamic-slice_fusion.6
  156.6 0.9 constant_dynamic-slice_fusion.6
  159.0 0.9 constant_dynamic-slice_fusion.6
  161.5 0.9 constant_dynamic-slice_fusion.6
  163.4 1.1 fusion.77
  164.6 72.9 %all-reduce.2.cloned.1.call-done = f32[96,1024]{1,0:T(8,128)} async-done(((f32[96,1024]{1,0:T(8,128)}), f32[96,1024]{1,0:T(8,128)}) %all-reduce.2.cloned.1.call-update) | async-done | bytes 393232 | tf_op jit(solution)/shard_map/psum | solution.py:120
  237.5 1.1 multiply_reduce_fusion
  238.9 1.2 fusion.78
  240.1 2.0 fusion.12
  242.1 1.3 copy.114
  243.5 1.4 reshape.204
  245.0 83.7 %reduce-scatter.4.cloned.1.call-done = f32[32,32]{1,0:T(8,128)} async-done(((f32[1024,32]{1,0:T(8,128)}), f32[32,32]{1,0:T(8,128)}) %reduce-scatter.4.cloned.1.call-update) | async-done | bytes 4112
  328.7 0.8 reshape.205
  329.6 1.6 stack.3
  331.2 4.3 reshape.206
  335.5 11.2 %all-to-all-start = ((bf16[256,2,512]{2,1,0:T(2,128)(2,1)}), bf16[256,2,512]{2,1,0:T(2,128)(2,1)S(1)}, u32[]{:S(2)}, u32[]{:S(2)}) async-start(bf16[256,2,512]{2,1,0:T(2,128)(2,1)} %reshape.206), calls=%async_computation | async-start | bytes 1048576 | tf_op jit(solution)/shard_map/all_to_all | solution.py:168
  347.4 20.0 %all-to-all-done = bf16[256,2,512]{2,1,0:T(2,128)(2,1)S(1)} async-done(((bf16[256,2,512]{2,1,0:T(2,128)(2,1)}), bf16[256,2,512]{2,1,0:T(2,128)(2,1)S(1)}, u32[]{:S(2)}, u32[]{:S(2)}) %all-to-all-start) | async-done | bytes 524320 | tf_op jit(solution)/shard_map/all_to_all | solution.py:168
  367.4 2.1 reshape.207
  369.5 4.2 copy.108
  373.7 3.5 reshape.187
  377.9 0.8 convolution_reduce_fusion
  378.7 63.6 %pmax.7 = f32[12]{0:T(128)} all-reduce(f32[12]{0:T(128)S(1)} %convolution_reduce_fusion), channel_id=1, replica_groups=mesh['seq'=32,'head'=8] {'seq'}, use_global_device_ids=true, to_apply=%region_15.16 | all-reduce | flops 12 | bytes 96 | tf_op jit(solution)/shard_map/pmax | solution.py:198
  (204 shorter events, 53.4 us)
Async XLA Ops:
  7.2 370.7 %copy-start = (bf16[1024,1004]{0,1:T(8,128)(2,1)S(1)}, bf16[1024,1004]{0,1:T(8,128)(2,1)}, u32[]{:S(2)}) copy-start(bf16[1024,1004]{0,1:T(8,128)(2,1)} %param.39) | copy-start | bytes 6168580
  7.2 4.8 %copy-start.2 = (bf16[96,1024]{1,0:T(8,128)(2,1)S(1)}, bf16[96,1024]{1,0:T(8,128)(2,1)}, u32[]{:S(2)}) copy-start(bf16[96,1024]{1,0:T(8,128)(2,1)} %param.21) | copy-start | bytes 589828
  7.2 4.8 %copy-start.12 = (f32[1024]{0:T(1024)S(1)}, f32[1024]{0:T(1024)}, u32[]{:S(2)}) copy-start(f32[1024]{0:T(1024)} %param.26) | copy-start | bytes 12292
  7.2 4.8 %copy-start.9 = (bf16[1024,128]{1,0:T(8,128)(2,1)S(1)}, bf16[1024,128]{1,0:T(8,128)(2,1)}, u32[]{:S(2)}) copy-start(bf16[1024,128]{1,0:T(8,128)(2,1)} %param.28) | copy-start | bytes 786436
  7.2 78.8 %all-gather.5.cloned.1.call-start = ((), (), s32[]{:S(2)}) async-start(), calls=%async_computation.3 | async-start | bytes 3244032 | tf_op jit(solution)/shard_map/all_gather | solution.py:10
  16.9 5.0 %copy-start.10 = (s32[24,4,512]{2,1,0:T(4,128)S(1)}, s32[24,4,512]{2,1,0:T(4,128)}, u32[]{:S(2)}) copy-start(s32[24,4,512]{2,1,0:T(4,128)} %param.25) | copy-start | bytes 589828
  17.0 5.0 %copy-start.14 = (f32[32,2]{0,1:T(2,128)S(1)}, f32[32,2]{0,1:T(2,128)}, u32[]{:S(2)}) copy-start(f32[32,2]{0,1:T(2,128)} %param.30) | copy-start | bytes 772
  24.0 3.1 copy-start.1
  28.8 3.3 copy-start.6
  32.1 205.4 %all-reduce.2.cloned.1.call-start = ((), (), s32[]{:S(2)}) async-start(), calls=%async_computation.2 | async-start | bytes 786432 | tf_op jit(solution)/shard_map/psum | solution.py:120
  59.1 104.3 %copy-start.4 = (bf16[128,1024]{1,0:T(8,128)(2,1)S(1)}, bf16[128,1024]{1,0:T(8,128)(2,1)}, u32[]{:S(2)}) copy-start(bf16[128,1024]{1,0:T(8,128)(2,1)} %param.31) | copy-start | bytes 786436
  86.9 151.7 %copy-start.13 = (f32[1024]{0:T(1024)S(1)}, f32[1024]{0:T(1024)}, u32[]{:S(2)}) copy-start(f32[1024]{0:T(1024)} %param.32) | copy-start | bytes 12292
  163.0 77.1 %copy-start.3 = (bf16[2,88,1024]{2,1,0:T(8,128)(2,1)S(1)}, bf16[2,88,1024]{2,1,0:T(8,128)(2,1)}, u32[]{:S(2)}) copy-start(bf16[2,88,1024]{2,1,0:T(8,128)(2,1)} %param.36) | copy-start | bytes 1081348
  164.5 164.2 %reduce-scatter.4.cloned.1.call-start = ((), (), s32[]{:S(2)}) async-start(), calls=%async_computation.4 | async-start | bytes 540672
  244.9 101.9 %copy-start.11 = (f32[1024,16]{0,1:T(8,128)S(1)}, f32[1024,16]{0,1:T(8,128)}, u32[]{:S(2)}) copy-start(f32[1024,16]{0,1:T(8,128)} %param.33) | copy-start | bytes 196612
  335.5 31.9 %all-to-all-start = ((bf16[256,2,512]{2,1,0:T(2,128)(2,1)}), bf16[256,2,512]{2,1,0:T(2,128)(2,1)S(1)}, u32[]{:S(2)}, u32[]{:S(2)}) async-start(bf16[256,2,512]{2,1,0:T(2,128)(2,1)} %reshape.206), calls=%async_computation | async-start | bytes 1048576 | tf_op jit(solution)/shard_map/all_to_all | solution.py:168
  369.5 8.4 %copy-start.7 = (f32[1024]{0:T(1024)S(1)}, f32[1024]{0:T(1024)}, u32[]{:S(2)}) copy-start(f32[1024]{0:T(1024)} %param.38) | copy-start | bytes 12292
  377.8 64.4 %copy-start.5 = (bf16[12,1024]{1,0:T(8,128)(2,1)}, bf16[12,1024]{1,0:T(8,128)(2,1)S(1)}, u32[]{:S(2)}) copy-start(bf16[12,1024]{1,0:T(8,128)(2,1)S(1)} %get-tuple-element.250) | copy-start | bytes 73732
  377.8 64.4 %copy-start.8 = (f32[12]{0:T(128)}, f32[12]{0:T(128)S(1)}, u32[]{:S(2)}) copy-start(f32[12]{0:T(128)S(1)} %add_sqrt_fusion) | copy-start | bytes 148
Sparse Core Ops, SparseCore 0:
  32.2 53.7 all-gather.4
  164.6 72.8 all-reduce.1
  245.0 83.6 reduce-scatter.3
